TPU v7x, 256 devices: a whole 4x4x8 slice. The times are simulated.
256 devices in a mesh: gx: 32 (over y, x, core), gy: 8 (over z).
Axes of the slice: x: 4, y: 4, z: 8, core: 2. Of those that a mesh axis runs over, the one named last changes fastest.
Arguments:
- displacement: float32 [3, 32, 256, 1024], P(None, None, 'gx', 'gy'), may hold values from -6 to 6
- velocity: float32 [3, 32, 256, 1024], P(None, None, 'gx', 'gy'), may hold values from -6 to 6
- slopes: float32 [2, 32, 256, 1024], P(None, None, 'gx', 'gy'), may hold values from -0.5 to 0.5
- stretch: float32 [32, 256, 1024], P(None, 'gx', 'gy'), may hold values from 0.6 to 1.4
- moduli: float32 [2, 32, 256, 1024], P(None, None, 'gx', 'gy'), may hold values from 0.3 to 1
- buoyancy: float32 [32, 256, 1024], P(None, 'gx', 'gy'), may hold values from 0.5 to 1.5
- probes: float32 [4, 512, 128], P(None, 'gy'), may hold values from -0.0017089844 to 0.0017089844
Outputs:
- final_displacement: float32 [3, 32, 256, 1024], P(None, None, 'gx', 'gy')
- basis: float32 [128, 48, 128], P('gx', 'gy')
- factor: float32 [128, 128], replicated
All inputs are finite; a program needn't handle non-finite values.
Results may differ from a plain program's by a relative error of at most 0.0003.
Values sent between devices are 32-bit elements; how exact they have to be, the bound alone decides.
A program may use at most 64 MiB of HBM per device.

v0:
```python
import math
import jax
import jax.numpy as jnp
from jax import lax
from jax.sharding import PartitionSpec as P

STEPS = 4
time_step = 0.12


def extended(block, sides, width):
    for axis, dim in sides:
        count = lax.axis_size(axis)
        forward = [(i, i + 1) for i in range(count - 1)]
        backward = [(target, source) for source, target in forward]
        low = lax.ppermute(
            lax.slice_in_dim(block, block.shape[dim] - width, None, axis=dim), axis, forward
        )
        high = lax.ppermute(lax.slice_in_dim(block, 0, width, axis=dim), axis, backward)
        block = jnp.concatenate([low, block, high], axis=dim)
    return block


def fourth(values, dimension):
    length_out = values.shape[dimension] - 4

    def segment(offset):
        return lax.slice_in_dim(values, offset, offset + length_out, axis=dimension)

    return (segment(0) - segment(4) + 8.0 * (segment(3) - segment(1))) / 12.0


def vertical(values):
    padded = jnp.pad(values, ((0, 0), (2, 2), (0, 0), (0, 0)))
    return fourth(padded, 1)


def gradient(padded, slope_x, slope_y, stretch):
    d_x = fourth(padded[:, :, :, 2:-2], 2)
    d_y = fourth(padded[:, :, 2:-2, :], 3)
    d_r = vertical(padded[:, :, 2:-2, 2:-2])
    return jnp.stack([d_x + slope_x * d_r, d_y + slope_y * d_r, stretch * d_r], axis=1)


def stresses(gradients, lame, shear):
    divergence = gradients[0, 0] + gradients[1, 1] + gradients[2, 2]
    pressure = lame * divergence
    return jnp.stack(
        [
            pressure + 2.0 * shear * gradients[0, 0],
            pressure + 2.0 * shear * gradients[1, 1],
            pressure + 2.0 * shear * gradients[2, 2],
            shear * (gradients[0, 1] + gradients[1, 0]),
            shear * (gradients[0, 2] + gradients[2, 0]),
            shear * (gradients[1, 2] + gradients[2, 1]),
        ]
    )


def forces(padded, slope_x, slope_y, stretch):
    d_x = fourth(padded[:, :, :, 2:-2], 2)
    d_y = fourth(padded[:, :, 2:-2, :], 3)
    d_r = vertical(padded[:, :, 2:-2, 2:-2])
    rows_x = (0, 3, 4)
    rows_y = (3, 1, 5)
    rows_z = (4, 5, 2)
    return jnp.stack(
        [
            d_x[rows_x[component]]
            + slope_x * d_r[rows_x[component]]
            + d_y[rows_y[component]]
            + slope_y * d_r[rows_y[component]]
            + stretch * d_r[rows_z[component]]
            for component in range(3)
        ]
    )


def lower_factor(gram):
    order = gram.shape[0]
    positions = jnp.arange(order, dtype=jnp.int32)

    def column_step(column_index, lower):
        picker = (positions == column_index).astype(jnp.float32)
        column = jnp.dot(gram, picker, precision=lax.Precision.HIGHEST)
        row_of = jnp.dot(picker, lower, precision=lax.Precision.HIGHEST)
        column = column - jnp.dot(lower, row_of, precision=lax.Precision.HIGHEST)
        pivot = jnp.sqrt(jnp.sum(column * picker))
        entries = jnp.where(
            positions > column_index,
            column / pivot,
            jnp.where(positions == column_index, pivot, 0.0),
        )
        return lower + entries[:, None] * picker[None, :]

    return lax.fori_loop(0, order, column_step, jnp.zeros_like(gram))


def lower_inverse(lower):
    order = lower.shape[0]
    positions = jnp.arange(order, dtype=jnp.int32)

    def row_step(row_index, inverse):
        picker = (positions == row_index).astype(jnp.float32)
        row_of = jnp.dot(picker, lower, precision=lax.Precision.HIGHEST)
        pivot = jnp.sum(row_of * picker)
        fresh = (picker - jnp.dot(row_of, inverse, precision=lax.Precision.HIGHEST)) / pivot
        return inverse + picker[:, None] * fresh[None, :]

    return lax.fori_loop(0, order, row_step, jnp.zeros_like(lower))


def orthogonalize(tall_block, gram):
    lower = lower_factor(gram)
    inverse = lower_inverse(lower)
    result = jnp.dot(
        tall_block, inverse.T, precision=lax.Precision.HIGHEST, preferred_element_type=jnp.float32
    )
    return (result, lower.T)


def shards(displacement, velocity, slopes, stretch, moduli, buoyancy, probes):
    previous = displacement - time_step * velocity
    current = displacement
    for moment in range(STEPS):
        padded = extended(current, (("gx", 2), ("gy", 3)), 2)
        gradients = gradient(padded, slopes[0], slopes[1], stretch)
        stress = extended(stresses(gradients, moduli[0], moduli[1]), (("gx", 2), ("gy", 3)), 2)
        pushes = buoyancy * forces(stress, slopes[0], slopes[1], stretch)
        following = 2.0 * current - previous + time_step**2 * pushes
        velocities = (following - previous) / (2.0 * time_step)
        sampled = velocities[:, ::2, ::2, ::2]
        half_x = sampled.shape[2]
        rearranged = jnp.transpose(sampled, (2, 0, 1, 3)).reshape(-1, sampled.shape[3])
        sketch_term = jnp.dot(
            rearranged,
            probes[moment],
            precision=lax.Precision.HIGHEST,
            preferred_element_type=jnp.float32,
        ).reshape(half_x, -1, probes.shape[2])
        reduced = lax.psum_scatter(sketch_term, "gy", scatter_dimension=1, tiled=True)
        sketch = reduced if moment == 0 else sketch + reduced
        previous, current = (current, following)
    tall_block = sketch.reshape(-1, sketch.shape[2])
    rows_total = tall_block.shape[0] * lax.axis_size("gx") * lax.axis_size("gy")
    gram_local = jnp.dot(
        tall_block.T,
        tall_block,
        precision=lax.Precision.HIGHEST,
        preferred_element_type=jnp.float32,
    )
    gram_whole = lax.psum(gram_local, ("gx", "gy"))
    orthonormal, factor = orthogonalize(tall_block, gram_whole)
    basis = (math.sqrt(rows_total) * orthonormal).reshape(sketch.shape)
    return (current, basis, factor)


def solution(mesh):
    in_specs = (
        P(None, None, "gx", "gy"),
        P(None, None, "gx", "gy"),
        P(None, None, "gx", "gy"),
        P(None, "gx", "gy"),
        P(None, None, "gx", "gy"),
        P(None, "gx", "gy"),
        P(None, "gy", None),
    )
    out_specs = (P(None, None, "gx", "gy"), P("gx", "gy", None), P())
    return jax.shard_map(shards, mesh=mesh, in_specs=in_specs, out_specs=out_specs, check_vma=False)
```

profile of v0, /device:TPU:1, one launch (start us, length us, event | category | flops | bytes accessed | tf_op | source)
XLA Modules:
  0.0 1194.3 jit_solution(5939340690643367252)
XLA Ops:
  8.8 4.6 collective-permute-start
  18.1 4.4 collective-permute-done.1
  26.6 4.9 collective-permute-start.2
  35.1 3.8 fusion.119
  49.6 4.4 collective-permute-done.5
  59.1 3.6 collective-permute-start.6
  76.9 3.5 collective-permute-start.8
  82.4 4.0 collective-permute-done.9
  89.0 3.7 collective-permute-start.10
  107.4 4.4 collective-permute-done.13
  117.2 5.1 collective-permute-start.14
  141.4 6.0 slice.1072
  150.9 3.6 collective-permute-start.18
  163.3 5.1 collective-permute-start.20
  171.9 6.0 slice.1074
  185.3 3.9 collective-permute-start.22
  202.2 5.1 collective-permute-start.24
  225.0 5.1 collective-permute-start.28
  233.0 4.0 collective-permute-done.29
  243.1 3.7 collective-permute-start.30
  266.5 78.0 %all-reduce.14.cloned.1.call-done = f32[4,48,128]{2,0,1:T(4,128)} async-done(((f32[4,48,128]{2,0,1:T(4,128)}), f32[4,48,128]{2,0,1:T(4,128)}) %all-reduce.14.cloned.1.call-update) | async-done | bytes 98320
  347.2 245.3 %all-reduce.12.cloned.1.call-done = f32[128,128]{1,0:T(8,128)} async-done(((f32[128,128]{1,0:T(8,128)}), f32[128,128]{1,0:T(8,128)}) %all-reduce.12.cloned.1.call-update) | async-done | bytes 65552 | tf_op jit(solution)/shard_map/psum | solution.py:152
  592.5 363.3 %while.30 = (s32[]{:T(128)}, f32[128,128]{1,0:T(8,128)S(1)}, f32[128,128]{1,0:T(8,128)}, s32[]{:T(128)}, s32[]{:T(128)}) while((s32[]{:T(128)}, f32[128,128]{1,0:T(8,128)S(1)}, f32[128,128]{1,0:T(8,128)}, s32[]{:T(128)}, s32[]{:T(128)}) %tuple.125), condition=%wide.region_7.8_spmd.clone.clone, body=%wide.region_5.7_spmd.clone.clone.sunk | while | flops 673410 | bytes 332917 | solution.py:96
  956.5 230.0 %while.29 = (s32[]{:T(128)}, f32[128,128]{1,0:T(8,128)S(1)}, f32[128,128]{1,0:T(8,128)S(1)}, s32[]{:T(128)}, s32[]{:T(128)}) while((s32[]{:T(128)}, f32[128,128]{1,0:T(8,128)S(1)}, f32[128,128]{1,0:T(8,128)S(1)}, s32[]{:T(128)}, s32[]{:T(128)}) %tuple.128), condition=%wide.region_10.11_spmd.clone, body=%wide.region_8.10_spmd.clone.sunk | while | flops 460034 | bytes 265316 | solution.py:110
  (1549 shorter events, 667.7 us)
Async XLA Ops:
  7.2 337.4 %all-reduce.14.cloned.1.call-start = ((), (), s32[]{:S(2)}) async-start(), calls=%async_computation.1 | async-start | bytes 196608
  8.8 9.3 collective-permute-start
  13.4 9.1 collective-permute-start.1
  25.3 16.2 %collective-permute-start.3 = (f32[3,32,12,2]{1,3,2,0:T(2,128)}, f32[3,32,12,2]{1,3,2,0:T(2,128)}, u32[]{:S(2)}, u32[]{:S(2)}) collective-permute-start(f32[3,32,12,2]{1,3,2,0:T(2,128)} %get-tuple-element.276), channel_id=1, source_target_pairs={{1,0},{2,1},{3,2},{4,3},{5,4},{6,5},{7,6},{9,8},{10,9},{11,10},{12... | collective-permute-start | bytes 27656 | tf_op jit(solution)/shard_map/ppermute | solution.py:19
  26.6 13.8 %collective-permute-start.2 = (f32[3,32,12,2]{1,3,2,0:T(2,128)}, f32[3,32,12,2]{1,3,2,0:T(2,128)}, u32[]{:S(2)}, u32[]{:S(2)}) collective-permute-start(f32[3,32,12,2]{1,3,2,0:T(2,128)} %get-tuple-element.277), channel_id=1, source_target_pairs={{0,1},{1,2},{2,3},{3,4},{4,5},{5,6},{6,7},{8,9},{9,10},{10,11},{11... | collective-permute-start | bytes 27656 | tf_op jit(solution)/shard_map/ppermute | solution.py:16
  47.0 7.0 collective-permute-start.5
  59.1 10.4 collective-permute-start.6
  80.4 5.9 collective-permute-start.9
  89.0 9.1 collective-permute-start.10
  104.8 7.0 collective-permute-start.13
  117.2 13.2 %collective-permute-start.14 = (f32[6,32,12,2]{1,3,2,0:T(2,128)S(1)}, f32[6,32,12,2]{1,3,2,0:T(2,128)S(1)}, u32[]{:S(2)}, u32[]{:S(2)}) collective-permute-start(f32[6,32,12,2]{1,3,2,0:T(2,128)S(1)} %copy.329), channel_id=1, source_target_pairs={{0,1},{1,2},{2,3},{3,4},{4,5},{5,6},{6,7},{8,9},{9,10},{10,11},{11... | collective-permute-start | bytes 55304 | tf_op jit(solution)/shard_map/ppermute | solution.py:16
  136.6 11.5 collective-permute-start.16
  139.5 8.6 collective-permute-start.17
  150.9 8.8 collective-permute-start.18
  163.3 15.3 %collective-permute-start.20 = (f32[6,32,2,128]{3,1,2,0:T(8,128)S(1)}, f32[6,32,2,128]{3,1,2,0:T(8,128)S(1)}, u32[]{:S(2)}, u32[]{:S(2)}) collective-permute-start(f32[6,32,2,128]{3,1,2,0:T(8,128)S(1)} %get-tuple-element.294), channel_id=1, source_target_pairs={{0,8},{8,16},{16,24},{24,32},{32,40},{40,48},{48,56},{56,64},{64,7... | collective-permute-start | bytes 589832 | tf_op jit(solution)/shard_map/ppermute | solution.py:16
  168.4 10.2 collective-permute-start.21
  185.3 11.0 collective-permute-start.22
  202.2 11.8 collective-permute-start.24
  207.3 6.7 collective-permute-start.25
  214.9 7.5 collective-permute-start.26
  225.0 8.0 collective-permute-start.28
  230.1 7.0 collective-permute-start.29
  243.1 11.6 collective-permute-start.30
  265.2 327.3 %all-reduce.12.cloned.1.call-start = ((), (), s32[]{:S(2)}) async-start(), calls=%async_computation | async-start | bytes 131072 | tf_op jit(solution)/shard_map/psum | solution.py:152
  (52 other events, 254.3 us)
Sparse Core Ops, SparseCore 0:
  265.3 79.1 all-reduce.13
  351.5 240.9 all-reduce.11
where the time goes:
time: 1210 us; the launch traced here: 1190 us
  matrix products  475 us (39%)
  waiting for transfers between devices  362 us (30%)
  loops' own time  98.3 us (8%)
  starting transfers between devices  89 us (7%)
  local copies, waits for them, and re-layouts  85.4 us (7%)
  other arithmetic  68.3 us (6%)
  between operations  15.9 us (1%)
    psum x1, waiting for transfers between devices, shards(): gram_whole = lax.psum(gram_local, ('gx', 'gy'))  245 us
    dot_general x128, matrix products, column_step(): column = jnp.dot(gram, picker, precision=lax.Precision.HIGHEST)  124 us
    dot_general x128, matrix products, column_step(): column = column - jnp.dot(lower, row_of, precision=lax.Precision.HIGHEST)  108 us
    dot_general x128, matrix products, row_step(): jnp.dot(row_of, inverse, precision=lax.Precision.HIGHEST)  107 us
    dot_general x128, matrix products, row_step(): row_of = jnp.dot(picker, lower, precision=lax.Precision.HIGHEST)  105 us
    another operation x1, loops' own time, lower_factor(): return lax.fori_loop(0, order, column_step, jnp.zeros_like(gram))  94 us
    unnamed x3, waiting for transfers between devices  78.1 us
    ppermute x16, starting transfers between devices, extended(): lax.ppermute(lax.slice_in_dim(block, block.shape[dim] - width, None, axis...  62.5 us
  transfers between devices with their start and end apart: 34, of which 17 were waited for; matrix products, arithmetic and copies ran while one was open for 5% of the time, Pallas kernels for 0%

commit v1 on v0

--- a/solution.py
+++ b/solution.py
@@ -149,7 +149,8 @@
         precision=lax.Precision.HIGHEST,
         preferred_element_type=jnp.float32,
     )
-    gram_whole = lax.psum(gram_local, ("gx", "gy"))
+    parts = lax.all_gather(gram_local, ("gx", "gy"), axis=0, tiled=False)
+    gram_whole = parts.sum(axis=0)
     orthonormal, factor = orthogonalize(tall_block, gram_whole)
     basis = (math.sqrt(rows_total) * orthonormal).reshape(sketch.shape)
     return (current, basis, factor)

time: 1210 us -> 966 us (0.80)
  matrix products: 475 us -> 352 us
  waiting for transfers between devices: 362 us -> 242 us
    psum x1 -> x0, waiting for transfers between devices: 245 us -> none  [shards(): gram_whole = lax.psum(gram_local, ('gx', 'gy'))]
    all_gather x0 -> x1, waiting for transfers between devices: none -> 130 us  [shards(): parts = lax.all_gather(gram_local, ('gx', 'gy'), axis=0, tiled=False)]
    dot_general x128, matrix products: 124 us -> 19 us  [column_step(): column = jnp.dot(gram, picker, precision=lax.Precision.HIGHEST)]
  transfers between devices with their start and end apart: 34 -> 34, of which waited for: 17 -> 16; matrix products, arithmetic and copies ran while one was open for 5% -> 6% of each run, Pallas kernels for 0% -> 0%
where the time goes in v1:
time: 966 us; the launch traced here: 960 us
  matrix products  352 us (36%)
  waiting for transfers between devices  242 us (25%)
  loops' own time  97.7 us (10%)
  starting transfers between devices  92.1 us (10%)
  local copies, waits for them, and re-layouts  86.6 us (9%)
  other arithmetic  73.9 us (8%)
  between operations  15.9 us (2%)
    all_gather x1, waiting for transfers between devices, shards(): parts = lax.all_gather(gram_local, ('gx', 'gy'), axis=0, tiled=False)  130 us
    dot_general x128, matrix products, column_step(): column = column - jnp.dot(lower, row_of, precision=lax.Precision.HIGHEST)  113 us
    dot_general x128, matrix products, row_step(): jnp.dot(row_of, inverse, precision=lax.Precision.HIGHEST)  98.2 us
    dot_general x128, matrix products, row_step(): row_of = jnp.dot(picker, lower, precision=lax.Precision.HIGHEST)  97.2 us
    another operation x1, loops' own time, lower_factor(): return lax.fori_loop(0, order, column_step, jnp.zeros_like(gram))  94 us
    unnamed x3, waiting for transfers between devices  79.7 us
    ppermute x16, starting transfers between devices, extended(): lax.ppermute(lax.slice_in_dim(block, block.shape[dim] - width, None, axis...  65.2 us
    ppermute x16, waiting for transfers between devices, extended(): lax.ppermute(lax.slice_in_dim(block, 0, width, axis=dim), axis, backward)  29.6 us
  transfers between devices with their start and end apart: 34, of which 16 were waited for; matrix products, arithmetic and copies ran while one was open for 6% of the time, Pallas kernels for 0%

profile of v1, /device:TPU:1, one launch (start us, length us, event | category | flops | bytes accessed | tf_op | source)
XLA Modules:
  0.0 959.9 jit_solution(8605386802294986912)
XLA Ops:
  8.8 4.6 collective-permute-start
  18.1 4.4 collective-permute-done.1
  25.3 4.1 collective-permute-start.2
  34.4 3.7 fusion.119
  48.7 4.4 collective-permute-done.5
  57.1 4.9 collective-permute-start.6
  81.4 4.0 collective-permute-done.9
  88.5 3.6 collective-permute-start.10
  108.0 4.4 collective-permute-done.13
  116.1 5.3 collective-permute-start.14
  140.5 6.0 slice.1072
  149.7 3.9 collective-permute-start.18
  162.7 6.1 collective-permute-start.20
  172.3 6.0 slice.1074
  184.4 3.9 collective-permute-start.22
  201.1 5.1 collective-permute-start.24
  213.5 3.7 collective-permute-start.26
  225.2 4.8 collective-permute-start.28
  240.7 3.6 collective-permute-start.30
  264.0 79.6 %all-reduce.11.cloned.1.call-done = f32[4,48,128]{2,0,1:T(4,128)} async-done(((f32[4,48,128]{2,0,1:T(4,128)}), f32[4,48,128]{2,0,1:T(4,128)}) %all-reduce.11.cloned.1.call-update) | async-done | bytes 98320
  346.3 130.4 %all-gather.3.cloned.1.call-done = f32[32768,128]{1,0:T(8,128)} async-done(((f32[128,128]{1,0:T(8,128)}), f32[32768,128]{1,0:T(8,128)}) %all-gather.3.cloned.1.call-update) | async-done | bytes 16777232 | tf_op jit(solution)/shard_map/all_gather | solution.py:152
  476.7 6.6 reduce_sum.35
  483.3 255.7 %while.30 = (s32[]{:T(128)}, f32[128,128]{1,0:T(8,128)S(1)}, f32[128,128]{1,0:T(8,128)S(1)}, s32[]{:T(128)}, s32[]{:T(128)}) while((s32[]{:T(128)}, f32[128,128]{1,0:T(8,128)S(1)}, f32[128,128]{1,0:T(8,128)S(1)}, s32[]{:T(128)}, s32[]{:T(128)}) %tuple.125), condition=%wide.region_7.8_spmd.clone.clone, body=%wide.region_5.7_spmd.clone.clone.sunk | while | flops 673410 | bytes 332909 | solution.py:96
  739.7 212.5 %while.29 = (s32[]{:T(128)}, f32[128,128]{1,0:T(8,128)S(1)}, f32[128,128]{1,0:T(8,128)S(1)}, s32[]{:T(128)}, s32[]{:T(128)}) while((s32[]{:T(128)}, f32[128,128]{1,0:T(8,128)S(1)}, f32[128,128]{1,0:T(8,128)S(1)}, s32[]{:T(128)}, s32[]{:T(128)}) %tuple.128), condition=%wide.region_10.11_spmd.clone, body=%wide.region_8.10_spmd.clone.sunk | while | flops 460034 | bytes 265308 | solution.py:110
  (1554 shorter events, 543.1 us)
Async XLA Ops:
  7.2 336.4 %all-reduce.11.cloned.1.call-start = ((), (), s32[]{:S(2)}) async-start(), calls=%async_computation.1 | async-start | bytes 196608
  8.8 9.3 collective-permute-start
  13.4 9.1 collective-permute-start.1
  25.3 14.3 %collective-permute-start.2 = (f32[3,32,12,2]{1,3,2,0:T(2,128)}, f32[3,32,12,2]{1,3,2,0:T(2,128)}, u32[]{:S(2)}, u32[]{:S(2)}) collective-permute-start(f32[3,32,12,2]{1,3,2,0:T(2,128)} %get-tuple-element.277), channel_id=1, source_target_pairs={{0,1},{1,2},{2,3},{3,4},{4,5},{5,6},{6,7},{8,9},{9,10},{10,11},{11... | collective-permute-start | bytes 27656 | tf_op jit(solution)/shard_map/ppermute | solution.py:16
  29.4 11.3 %collective-permute-start.3 = (f32[3,32,12,2]{1,3,2,0:T(2,128)}, f32[3,32,12,2]{1,3,2,0:T(2,128)}, u32[]{:S(2)}, u32[]{:S(2)}) collective-permute-start(f32[3,32,12,2]{1,3,2,0:T(2,128)} %get-tuple-element.276), channel_id=1, source_target_pairs={{1,0},{2,1},{3,2},{4,3},{5,4},{6,5},{7,6},{9,8},{10,9},{11,10},{12... | collective-permute-start | bytes 27656 | tf_op jit(solution)/shard_map/ppermute | solution.py:19
  46.1 7.0 collective-permute-start.5
  57.1 10.0 %collective-permute-start.6 = (f32[6,32,12,2]{1,3,2,0:T(2,128)S(1)}, f32[6,32,12,2]{1,3,2,0:T(2,128)}, u32[]{:S(2)}, u32[]{:S(2)}) collective-permute-start(f32[6,32,12,2]{1,3,2,0:T(2,128)S(1)} %copy.317), channel_id=1, source_target_pairs={{0,1},{1,2},{2,3},{3,4},{4,5},{5,6},{6,7},{8,9},{9,10},{10,11},{11... | collective-permute-start | bytes 55304 | tf_op jit(solution)/shard_map/ppermute | solution.py:16
  79.5 5.9 collective-permute-start.9
  88.5 7.0 collective-permute-start.10
  105.4 7.0 collective-permute-start.13
  116.1 10.2 %collective-permute-start.14 = (f32[6,32,12,2]{1,3,2,0:T(2,128)S(1)}, f32[6,32,12,2]{1,3,2,0:T(2,128)S(1)}, u32[]{:S(2)}, u32[]{:S(2)}) collective-permute-start(f32[6,32,12,2]{1,3,2,0:T(2,128)S(1)} %copy.329), channel_id=1, source_target_pairs={{0,1},{1,2},{2,3},{3,4},{4,5},{5,6},{6,7},{8,9},{9,10},{10,11},{11... | collective-permute-start | bytes 55304 | tf_op jit(solution)/shard_map/ppermute | solution.py:16
  135.6 11.6 %collective-permute-start.16 = (f32[3,32,2,128]{3,1,2,0:T(8,128)S(1)}, f32[3,32,2,128]{3,1,2,0:T(8,128)S(1)}, u32[]{:S(2)}, u32[]{:S(2)}) collective-permute-start(f32[3,32,2,128]{3,1,2,0:T(8,128)S(1)} %get-tuple-element.316), channel_id=1, source_target_pairs={{0,8},{8,16},{16,24},{24,32},{32,40},{40,48},{48,56},{56,64},{64,7... | collective-permute-start | bytes 294920 | tf_op jit(solution)/shard_map/ppermute | solution.py:16
  138.6 8.6 collective-permute-start.17
  149.7 6.7 collective-permute-start.18
  162.7 16.3 %collective-permute-start.20 = (f32[6,32,2,128]{3,1,2,0:T(8,128)S(1)}, f32[6,32,2,128]{3,1,2,0:T(8,128)S(1)}, u32[]{:S(2)}, u32[]{:S(2)}) collective-permute-start(f32[6,32,2,128]{3,1,2,0:T(8,128)S(1)} %get-tuple-element.294), channel_id=1, source_target_pairs={{0,8},{8,16},{16,24},{24,32},{32,40},{40,48},{48,56},{56,64},{64,7... | collective-permute-start | bytes 589832 | tf_op jit(solution)/shard_map/ppermute | solution.py:16
  168.8 10.2 %collective-permute-start.21 = (f32[6,32,2,128]{3,1,2,0:T(8,128)S(1)}, f32[6,32,2,128]{3,1,2,0:T(8,128)S(1)}, u32[]{:S(2)}, u32[]{:S(2)}) collective-permute-start(f32[6,32,2,128]{3,1,2,0:T(8,128)S(1)} %get-tuple-element.295), channel_id=1, source_target_pairs={{8,0},{16,8},{24,16},{32,24},{40,32},{48,40},{56,48},{64,56},{72,6... | collective-permute-start | bytes 589832 | tf_op jit(solution)/shard_map/ppermute | solution.py:19
  184.4 9.2 collective-permute-start.22
  201.1 11.8 %collective-permute-start.24 = (f32[3,32,2,128]{3,1,2,0:T(8,128)S(1)}, f32[3,32,2,128]{3,1,2,0:T(8,128)S(1)}, u32[]{:S(2)}, u32[]{:S(2)}) collective-permute-start(f32[3,32,2,128]{3,1,2,0:T(8,128)S(1)} %get-tuple-element.312), channel_id=1, source_target_pairs={{0,8},{8,16},{16,24},{24,32},{32,40},{40,48},{48,56},{56,64},{64,7... | collective-permute-start | bytes 294920 | tf_op jit(solution)/shard_map/ppermute | solution.py:16
  206.2 6.8 collective-permute-start.25
  213.5 6.8 collective-permute-start.26
  225.2 8.4 collective-permute-start.28
  230.0 7.0 collective-permute-start.29
  240.7 8.7 collective-permute-start.30
  262.7 214.0 %all-gather.3.cloned.1.call-start = ((), (), s32[]{:S(2)}) async-start(), calls=%async_computation | async-start | bytes 16842752 | tf_op jit(solution)/shard_map/all_gather | solution.py:152
  (54 other events, 253.5 us)
Sparse Core Ops, SparseCore 0:
  262.8 80.7 all-reduce.10
  348.4 128.2 all-gather.2
